TPU v7x, 512 devices: a whole 4x4x16 slice. The times are simulated.
512 devices in a mesh: orig: 32 (over z_lo, x, core), dest: 16 (over y, z_hi).
Axes of the slice: x: 4, y: 4, z: 16 (z_hi: 4, z_lo: 4; z = z_hi * 4 + z_lo), core: 2. Of those that a mesh axis runs over, the one named last changes fastest.
Arguments:
- pair_field: bfloat16 [1024, 1024, 128], P('orig', 'dest'), may hold values from -6 to 6
- region_mask: int32 [1024], replicated, may hold values 0 or 1
- region_count: int32 [1], replicated, may hold values from 1 to 1024
- row_query: bfloat16 [1, 128, 128], replicated, may hold values from -17.5 to 17.5, as said below
- row_key: bfloat16 [1, 128, 128], replicated, may hold values from -0.36 to 0.36, as said below
- row_value: bfloat16 [1, 128, 128], replicated, may hold values from -0.5 to 0.5
- row_gate: bfloat16 [1, 128, 128], replicated, may hold values from -0.5 to 0.5
- row_gate_bias: float32 [1, 128], replicated, may hold values from -4 to 4
- row_out: bfloat16 [1, 128, 128], replicated, may hold values from -1.5 to 1.5
- col_query: bfloat16 [1, 128, 128], replicated, may hold values from -17.5 to 17.5, as said below
- col_key: bfloat16 [1, 128, 128], replicated, may hold values from -0.36 to 0.36, as said below
- col_value: bfloat16 [1, 128, 128], replicated, may hold values from -0.5 to 0.5
- col_gate: bfloat16 [1, 128, 128], replicated, may hold values from -0.5 to 0.5
- col_gate_bias: float32 [1, 128], replicated, may hold values from -4 to 4
- col_out: bfloat16 [1, 128, 128], replicated, may hold values from -1.5 to 1.5
Outputs:
- new_pair: bfloat16 [1024, 1024, 128], P('orig', 'dest')
Inputs may be any that keep to these rules, and one draw needn't show every extreme that they name: `row_query`: row attention query weights. `row_key`: row attention key weights. `col_query`: column attention query weights. `col_key`: column attention key weights.
All inputs are finite; a program needn't handle non-finite values.
Results may differ from a plain program's by a relative error of at most 0.012.
Values may be sent and summed in bfloat16 or wider, within the bound.
A program may use at most 64 MiB of HBM per device.

v0:
```python
import math

import jax
import jax.numpy as jnp
from jax import lax
from jax.sharding import Mesh
from jax.sharding import PartitionSpec as P

H = 4
ORIG = ("orig_0", "orig_1", "orig_2")
ORIG_DEST = ("orig_0", "orig_1", "orig_2", "dest")


epsilon = 1e-05
masked_score = -1e30


def items_in_groups(x, axis, split_dim, concat_dim, work, item_dim, out_dim):
    items = jax.tree.leaves(x)[0].shape[item_dim]
    count = 2 if items % 2 == 0 else 1
    finished = []
    for k in range(count):
        group = jax.tree.map(
            lambda a: lax.slice_in_dim(
                a, k * (items // count), (k + 1) * (items // count), axis=item_dim
            ),
            x,
        )
        finished.append(
            work(
                lax.all_to_all(
                    group, axis, split_axis=split_dim, concat_axis=concat_dim, tiled=True
                )
            )
        )
    return jax.tree.map(lambda *parts: jnp.concatenate(parts, axis=out_dim), *finished)


def in_blocks(x, dim, size):
    shape = x.shape
    parts = x.reshape(*shape[:dim], size, shape[dim] // size, *shape[dim + 1 :])
    return jnp.moveaxis(parts, dim, 0)


def laid_out(parts, dim):
    shape = list(parts.shape[1:])
    shape[dim] *= parts.shape[0]
    return jnp.moveaxis(parts, 0, dim).reshape(shape)


def one_exchange(x, axis, axes, splits, concats):
    sizes = [lax.axis_size(a) for a in axes]
    parts = in_blocks(x, splits[0], sizes[0])
    parts = jnp.moveaxis(in_blocks(parts, splits[1] + 1, sizes[1]), 0, 1)
    inside = parts.shape[2:]
    parts = parts.reshape(-1, *inside)
    parts = lax.all_to_all(parts, axis, split_axis=0, concat_axis=0, tiled=True)
    parts = laid_out(parts.reshape(*sizes, *inside), concats[0] + 1)
    return laid_out(parts, concats[1])


def moved_by_axis(parts, axes, order):
    inside = parts.shape[1:]
    whole = parts.reshape(*(lax.axis_size(a) for a in axes), *inside)
    for k in order:
        whole = lax.all_to_all(whole, axes[k], k, k, tiled=True)
    return whole.reshape(-1, *inside)


def core_and_chips(x, groups, order, split_dim, concat_dim):
    size = lax.axis_size(groups[0]) * lax.axis_size(groups[1])
    parts = in_blocks(x, split_dim, size)
    return laid_out(moved_by_axis(parts, groups, order), concat_dim)


def normalize(pair_rows):
    widened = pair_rows.astype(jnp.float32)
    centered = widened - jnp.mean(widened, axis=-1, keepdims=True)
    variance = jnp.mean(centered * centered, axis=-1, keepdims=True)
    return (centered * lax.rsqrt(variance + epsilon)).astype(jnp.bfloat16)


def attend_heads(queries, key_rows, value_rows, valid_keys):
    items, length, channels = queries.shape
    head_size = channels // H
    block = min(512, length)
    count = length // block

    def heads_first(values):
        return jnp.transpose(values.reshape(items, length, H, head_size), (0, 2, 1, 3))

    query_heads = heads_first(queries).reshape(items * H, count, block, head_size)
    key_heads = heads_first(key_rows).reshape(items * H, length, head_size)
    value_heads = heads_first(value_rows).reshape(items * H, length, head_size)

    def one_head(operands):
        head_queries, head_keys, head_values = operands

        def one_block(block_queries):
            scores = jnp.einsum(
                "qd,kd->qk", block_queries, head_keys, preferred_element_type=jnp.float32
            ) / math.sqrt(head_size)
            scores = jnp.where(valid_keys[None, :], scores, masked_score)
            maximum = jnp.max(scores, axis=1, keepdims=True)
            expanded = jnp.exp(scores - maximum)
            weights = (expanded / jnp.sum(expanded, axis=1, keepdims=True)).astype(jnp.bfloat16)
            return jnp.dot(weights, head_values, preferred_element_type=jnp.float32).astype(
                jnp.bfloat16
            )

        return lax.map(one_block, head_queries)

    results = lax.map(one_head, (query_heads, key_heads, value_heads))
    return jnp.transpose(results.reshape(items, H, length, head_size), (0, 2, 1, 3)).reshape(
        items, length, channels
    )


def finish(pair_tile, normed, attended, w_gate, gate_bias, w_out, gate_form, out_form):
    gate_values = jax.nn.sigmoid(
        jnp.einsum(gate_form, normed, w_gate, preferred_element_type=jnp.float32) + gate_bias
    )
    gated = (gate_values * attended.astype(jnp.float32)).astype(jnp.bfloat16)
    update = jnp.einsum(out_form, gated, w_out, preferred_element_type=jnp.float32).reshape(
        pair_tile.shape
    )
    return (pair_tile.astype(jnp.float32) + update).astype(jnp.bfloat16)


def attend_pairs(pair_rows, weights, valid_keys):
    w_query, w_key, w_value, w_gate, gate_bias, w_out = weights
    normed = normalize(pair_rows)
    stacked = jnp.stack((w_query, w_key, w_value))
    projected = jnp.einsum(
        "nrc,scm->snrm", normed, stacked, preferred_element_type=jnp.float32
    ).astype(jnp.bfloat16)
    attended = attend_heads(projected[0], projected[1], projected[2], valid_keys)
    return finish(
        pair_rows, normed, attended, w_gate, gate_bias, w_out, "nrc,cm->nrm", "nrm,mc->nrc"
    )


def body(
    pair_field,
    region_mask,
    region_count,
    row_query,
    row_key,
    row_value,
    row_gate,
    row_gate_bias,
    row_out,
    col_query,
    col_key,
    col_value,
    col_gate,
    col_gate_bias,
    col_out,
):
    tile_rows, tile_cols, channels = pair_field.shape
    dest_size = lax.axis_size("dest")
    orig_size = lax.axis_size(ORIG)
    region_total = region_mask.shape[0]
    row_part = tile_rows // dest_size
    col_part = tile_cols // orig_size
    positions = jnp.arange(region_total, dtype=jnp.int32)
    valid_keys = ((region_mask == 1) | (positions == 0)) & (positions < region_count[0])
    current = pair_field
    row_weights = (
        row_query[0],
        row_key[0],
        row_value[0],
        row_gate[0],
        row_gate_bias[0],
        row_out[0],
    )
    col_weights = (
        col_query[0],
        col_key[0],
        col_value[0],
        col_gate[0],
        col_gate_bias[0],
        col_out[0],
    )

    def row_local(exchanged):
        return attend_pairs(exchanged[0], row_weights, valid_keys)[None]

    pieces = current.reshape(dest_size, row_part, tile_cols, channels)
    rows_whole = items_in_groups(pieces, "dest", 0, 2, row_local, 1, 1)
    spread = rows_whole.reshape(1, 1, row_part, dest_size, orig_size, col_part, channels)
    columns = one_exchange(spread, ORIG_DEST, (ORIG, "dest"), (4, 3), (0, 1))
    column_columns = columns.reshape(region_total, col_part, channels)
    updated = jnp.swapaxes(
        attend_pairs(jnp.swapaxes(column_columns, 0, 1), col_weights, valid_keys), 0, 1
    )
    back = core_and_chips(
        updated.reshape(region_total, 1, col_part, channels),
        (("orig_0", "orig_1"), "orig_2"),
        (1, 0),
        0,
        1,
    )
    current = back.reshape(tile_rows, tile_cols, channels)
    return current


def solution(mesh):
    split = Mesh(
        mesh.devices.reshape(4, 4, 2, mesh.shape["dest"]), ("orig_0", "orig_1", "orig_2", "dest")
    )
    return jax.shard_map(
        body,
        mesh=split,
        in_specs=(
            P(ORIG, "dest", None),
            P(),
            P(),
            P(),
            P(),
            P(),
            P(),
            P(),
            P(),
            P(),
            P(),
            P(),
            P(),
            P(),
            P(),
        ),
        out_specs=P(ORIG, "dest", None),
        check_vma=False,
    )
```

profile of v0, /device:TPU:1, one launch (start us, length us, event | category | flops | bytes accessed | tf_op | source)
XLA Modules:
  0.0 232.5 jit_solution(11939409782287132563)
XLA Ops:
  1.9 18.4 %all-to-all-start = ((bf16[16,1,64,128]{3,2,1,0:T(8,128)(2,1)}), bf16[16,1,64,128]{3,2,1,0:T(8,128)(2,1)S(1)}, u32[]{:S(2)}, u32[]{:S(2)}) async-start(bf16[16,1,64,128]{3,2,1,0:T(8,128)(2,1)} %get-tuple-element.293), calls=%async_computation | async-start | bytes 524288 | tf_op jit(solution)/shard_map/all_to_all | solution.py:31
  24.2 15.9 %all-to-all-done = bf16[16,1,64,128]{3,2,1,0:T(8,128)(2,1)S(1)} async-done(((bf16[16,1,64,128]{3,2,1,0:T(8,128)(2,1)}), bf16[16,1,64,128]{3,2,1,0:T(8,128)(2,1)S(1)}, u32[]{:S(2)}, u32[]{:S(2)}) %all-to-all-start) | async-done | bytes 262176 | tf_op jit(solution)/shard_map/all_to_all | solution.py:31
  47.5 18.6 %while.61 = (s32[]{:T(128)}, bf16[4,2,512,32]{2,3,1,0:T(8,128)(2,1)S(1)}, bf16[4,2,512,32]{3,2,1,0:T(8,128)(2,1)S(1)}, bf16[4,1024,32]{2,1,0:T(8,128)(2,1)S(1)},...) while((s32[]{:T(128)}, ...), condition=%wide.region_7.8_spmd, body=%wide.region_2.7_spmd.sunk | while | flops 73415680 | bytes 7517438 | solution.py:113
  48.6 3.6 %while.66 = (s32[]{:T(128)}, bf16[2,512,32]{1,2,0:T(8,128)(2,1)S(1)}, pred[1024]{0:T(1024)(128)(4,1)S(1)}, bf16[2,512,32]{2,1,0:T(8,128)(2,1)S(1)}, bf16[1024,32...) while((s32[]{:T(128)}, bf16[2,512,32]{1,2,0:T(8,128)(2,1)S(1)}, ...), condition=%wide.region_6.6_spmd, body=%wide.region_3.5_spmd.sunk | while | flops 73415680 | bytes 6992981 | solution.py:111
  53.2 3.6 %while.66 = (s32[]{:T(128)}, bf16[2,512,32]{1,2,0:T(8,128)(2,1)S(1)}, pred[1024]{0:T(1024)(128)(4,1)S(1)}, bf16[2,512,32]{2,1,0:T(8,128)(2,1)S(1)}, bf16[1024,32...) while((s32[]{:T(128)}, bf16[2,512,32]{1,2,0:T(8,128)(2,1)S(1)}, ...), condition=%wide.region_6.6_spmd, body=%wide.region_3.5_spmd.sunk | while | flops 73415680 | bytes 6992981 | solution.py:111
  57.9 3.6 %while.66 = (s32[]{:T(128)}, bf16[2,512,32]{1,2,0:T(8,128)(2,1)S(1)}, pred[1024]{0:T(1024)(128)(4,1)S(1)}, bf16[2,512,32]{2,1,0:T(8,128)(2,1)S(1)}, bf16[1024,32...) while((s32[]{:T(128)}, bf16[2,512,32]{1,2,0:T(8,128)(2,1)S(1)}, ...), condition=%wide.region_6.6_spmd, body=%wide.region_3.5_spmd.sunk | while | flops 73415680 | bytes 6992981 | solution.py:111
  62.5 3.6 %while.66 = (s32[]{:T(128)}, bf16[2,512,32]{1,2,0:T(8,128)(2,1)S(1)}, pred[1024]{0:T(1024)(128)(4,1)S(1)}, bf16[2,512,32]{2,1,0:T(8,128)(2,1)S(1)}, bf16[1024,32...) while((s32[]{:T(128)}, bf16[2,512,32]{1,2,0:T(8,128)(2,1)S(1)}, ...), condition=%wide.region_6.6_spmd, body=%wide.region_3.5_spmd.sunk | while | flops 73415680 | bytes 6992981 | solution.py:111
  72.2 18.6 %while.63 = (s32[]{:T(128)}, bf16[4,2,512,32]{2,3,1,0:T(8,128)(2,1)S(1)}, bf16[4,2,512,32]{3,2,1,0:T(8,128)(2,1)S(1)}, bf16[4,1024,32]{2,1,0:T(8,128)(2,1)S(1)},...) while((s32[]{:T(128)}, ...), condition=%wide.region_15.16_spmd, body=%wide.region_10.15_spmd.sunk | while | flops 73415680 | bytes 7517438 | solution.py:113
  73.3 3.6 %while.67 = (s32[]{:T(128)}, bf16[2,512,32]{1,2,0:T(8,128)(2,1)S(1)}, pred[1024]{0:T(1024)(128)(4,1)S(1)}, bf16[2,512,32]{2,1,0:T(8,128)(2,1)S(1)}, bf16[1024,32...) while((s32[]{:T(128)}, bf16[2,512,32]{1,2,0:T(8,128)(2,1)S(1)}, ...), condition=%wide.region_14.14_spmd, body=%wide.region_11.13_spmd.sunk | while | flops 73415680 | bytes 6992981 | solution.py:111
  82.6 3.6 %while.67 = (s32[]{:T(128)}, bf16[2,512,32]{1,2,0:T(8,128)(2,1)S(1)}, pred[1024]{0:T(1024)(128)(4,1)S(1)}, bf16[2,512,32]{2,1,0:T(8,128)(2,1)S(1)}, bf16[1024,32...) while((s32[]{:T(128)}, bf16[2,512,32]{1,2,0:T(8,128)(2,1)S(1)}, ...), condition=%wide.region_14.14_spmd, body=%wide.region_11.13_spmd.sunk | while | flops 73415680 | bytes 6992981 | solution.py:111
  87.2 3.6 %while.67 = (s32[]{:T(128)}, bf16[2,512,32]{1,2,0:T(8,128)(2,1)S(1)}, pred[1024]{0:T(1024)(128)(4,1)S(1)}, bf16[2,512,32]{2,1,0:T(8,128)(2,1)S(1)}, bf16[1024,32...) while((s32[]{:T(128)}, bf16[2,512,32]{1,2,0:T(8,128)(2,1)S(1)}, ...), condition=%wide.region_14.14_spmd, body=%wide.region_11.13_spmd.sunk | while | flops 73415680 | bytes 6992981 | solution.py:111
  94.1 23.6 %all-to-all-start.2 = ((bf16[512,1,1,2,1,1,2,128]{7,6,3,5,4,2,1,0:T(2,128)(2,1)}), bf16[512,1,1,2,1,1,2,128]{7,6,3,5,4,2,1,0:T(2,128)(2,1)S(1)}, u32[]{:S(2)}, u32[]{:S(2)}) async-start(bf16[512,1,1,2,1,1,2,128]{7,6,3,5,4,2,1,0:T(2,128)(2,1)} %copy.101), calls=%async_computation.2 | async-start | bytes 1048576 | tf_op jit(solution)/shard_map/all_to_all | solution.py:57
  118.0 34.3 %all-to-all-done.2 = bf16[512,1,1,2,1,1,2,128]{7,6,3,5,4,2,1,0:T(2,128)(2,1)S(1)} async-done(((bf16[512,1,1,2,1,1,2,128]{7,6,3,5,4,2,1,0:T(2,128)(2,1)}), bf16[512,1,1,2,1,1,2,128]{7,6,3,5,4,2,1,0:T(2,128)(2,1)S(1)}, u32[]{:S(2)}, u32[]{:S(2)}) %all-to-all-start.2) | async-done | bytes 524320 | tf_op jit(solution)/shard_map/all_to_all | solution.py:57
  160.8 45.4 %while.65 = (s32[]{:T(128)}, bf16[8,2,512,32]{2,3,1,0:T(8,128)(2,1)S(1)}, bf16[8,2,512,32]{3,2,1,0:T(8,128)(2,1)}, bf16[8,1024,32]{2,1,0:T(8,128)(2,1)}, bf16[8,...) while((s32[]{:T(128)}, ...), condition=%wide.region_23.24_spmd, body=%wide.region_18.23_spmd.sunk | while | flops 73415680 | bytes 7517438 | solution.py:113
  162.8 3.6 %while.68 = (s32[]{:T(128)}, bf16[2,512,32]{1,2,0:T(8,128)(2,1)S(1)}, pred[1024]{0:T(1024)(128)(4,1)S(1)}, bf16[2,512,32]{2,1,0:T(8,128)(2,1)S(1)}, bf16[1024,32...) while((s32[]{:T(128)}, bf16[2,512,32]{1,2,0:T(8,128)(2,1)S(1)}, ...), condition=%wide.region_22.22_spmd, body=%wide.region_19.21_spmd.sunk | while | flops 73415680 | bytes 6992981 | solution.py:111
  168.5 3.6 %while.68 = (s32[]{:T(128)}, bf16[2,512,32]{1,2,0:T(8,128)(2,1)S(1)}, pred[1024]{0:T(1024)(128)(4,1)S(1)}, bf16[2,512,32]{2,1,0:T(8,128)(2,1)S(1)}, bf16[1024,32...) while((s32[]{:T(128)}, bf16[2,512,32]{1,2,0:T(8,128)(2,1)S(1)}, ...), condition=%wide.region_22.22_spmd, body=%wide.region_19.21_spmd.sunk | while | flops 73415680 | bytes 6992981 | solution.py:111
  174.2 3.6 %while.68 = (s32[]{:T(128)}, bf16[2,512,32]{1,2,0:T(8,128)(2,1)S(1)}, pred[1024]{0:T(1024)(128)(4,1)S(1)}, bf16[2,512,32]{2,1,0:T(8,128)(2,1)S(1)}, bf16[1024,32...) while((s32[]{:T(128)}, bf16[2,512,32]{1,2,0:T(8,128)(2,1)S(1)}, ...), condition=%wide.region_22.22_spmd, body=%wide.region_19.21_spmd.sunk | while | flops 73415680 | bytes 6992981 | solution.py:111
  179.8 3.6 %while.68 = (s32[]{:T(128)}, bf16[2,512,32]{1,2,0:T(8,128)(2,1)S(1)}, pred[1024]{0:T(1024)(128)(4,1)S(1)}, bf16[2,512,32]{2,1,0:T(8,128)(2,1)S(1)}, bf16[1024,32...) while((s32[]{:T(128)}, bf16[2,512,32]{1,2,0:T(8,128)(2,1)S(1)}, ...), condition=%wide.region_22.22_spmd, body=%wide.region_19.21_spmd.sunk | while | flops 73415680 | bytes 6992981 | solution.py:111
  185.5 3.6 %while.68 = (s32[]{:T(128)}, bf16[2,512,32]{1,2,0:T(8,128)(2,1)S(1)}, pred[1024]{0:T(1024)(128)(4,1)S(1)}, bf16[2,512,32]{2,1,0:T(8,128)(2,1)S(1)}, bf16[1024,32...) while((s32[]{:T(128)}, bf16[2,512,32]{1,2,0:T(8,128)(2,1)S(1)}, ...), condition=%wide.region_22.22_spmd, body=%wide.region_19.21_spmd.sunk | while | flops 73415680 | bytes 6992981 | solution.py:111
  191.2 3.6 %while.68 = (s32[]{:T(128)}, bf16[2,512,32]{1,2,0:T(8,128)(2,1)S(1)}, pred[1024]{0:T(1024)(128)(4,1)S(1)}, bf16[2,512,32]{2,1,0:T(8,128)(2,1)S(1)}, bf16[1024,32...) while((s32[]{:T(128)}, bf16[2,512,32]{1,2,0:T(8,128)(2,1)S(1)}, ...), condition=%wide.region_22.22_spmd, body=%wide.region_19.21_spmd.sunk | while | flops 73415680 | bytes 6992981 | solution.py:111
  196.9 3.6 %while.68 = (s32[]{:T(128)}, bf16[2,512,32]{1,2,0:T(8,128)(2,1)S(1)}, pred[1024]{0:T(1024)(128)(4,1)S(1)}, bf16[2,512,32]{2,1,0:T(8,128)(2,1)S(1)}, bf16[1024,32...) while((s32[]{:T(128)}, bf16[2,512,32]{1,2,0:T(8,128)(2,1)S(1)}, ...), condition=%wide.region_22.22_spmd, body=%wide.region_19.21_spmd.sunk | while | flops 73415680 | bytes 6992981 | solution.py:111
  202.5 3.6 %while.68 = (s32[]{:T(128)}, bf16[2,512,32]{1,2,0:T(8,128)(2,1)S(1)}, pred[1024]{0:T(1024)(128)(4,1)S(1)}, bf16[2,512,32]{2,1,0:T(8,128)(2,1)S(1)}, bf16[1024,32...) while((s32[]{:T(128)}, bf16[2,512,32]{1,2,0:T(8,128)(2,1)S(1)}, ...), condition=%wide.region_22.22_spmd, body=%wide.region_19.21_spmd.sunk | while | flops 73415680 | bytes 6992981 | solution.py:111
  208.9 4.2 %all_to_all.33 = bf16[16,2,32,1,2,128]{5,2,0,4,3,1:T(8,128)(2,1)S(1)} all-to-all(bf16[16,2,32,1,2,128]{5,2,0,4,3,1:T(8,128)(2,1)S(1)} %copy.111), channel_id=1, replica_groups=mesh['orig_0'=4,'orig_1'=4,'orig_2'=2,'dest'=16] {'orig_2'}, dimensions={1} | all-to-all | bytes 1048576 | tf_op jit(solution)/shard_map/all_to_all | solution.py:66
  213.2 18.2 %all_to_all.34 = bf16[16,2,32,1,2,128]{5,2,1,4,3,0:T(8,128)(2,1)S(1)} all-to-all(bf16[16,2,32,1,2,128]{5,2,1,4,3,0:T(8,128)(2,1)S(1)} %copy.112), channel_id=1, replica_groups=mesh['orig_0'=4,'orig_1'=4,'orig_2'=2,'dest'=16] {'orig_0','orig_1'}, dimensions={0} | all-to-all | bytes 1048576 | tf_op jit(solution)/shard_map/all_to_all | solution.py:66
  (264 shorter events, 119.1 us)
Async XLA Ops:
  0.0 67.1 %copy-start = (bf16[1,128,128]{2,1,0:T(8,128)(2,1)S(1)}, bf16[1,128,128]{2,1,0:T(8,128)(2,1)}, u32[]{:S(2)}) copy-start(bf16[1,128,128]{2,1,0:T(8,128)(2,1)} %param.35) | copy-start | bytes 98308
  1.9 38.3 %all-to-all-start = ((bf16[16,1,64,128]{3,2,1,0:T(8,128)(2,1)}), bf16[16,1,64,128]{3,2,1,0:T(8,128)(2,1)S(1)}, u32[]{:S(2)}, u32[]{:S(2)}) async-start(bf16[16,1,64,128]{3,2,1,0:T(8,128)(2,1)} %get-tuple-element.293), calls=%async_computation | async-start | bytes 524288 | tf_op jit(solution)/shard_map/all_to_all | solution.py:31
  22.0 23.2 %copy-start.5 = (bf16[1,128,128]{1,2,0:T(8,128)(2,1)}, bf16[1,128,128]{1,2,0:T(8,128)(2,1)S(1)}, u32[]{:S(2)}) copy-start(bf16[1,128,128]{1,2,0:T(8,128)(2,1)S(1)} %copy.87) | copy-start | bytes 98308
  22.9 22.3 %copy-start.7 = (bf16[1,128,128]{1,2,0:T(8,128)(2,1)}, bf16[1,128,128]{1,2,0:T(8,128)(2,1)S(1)}, u32[]{:S(2)}) copy-start(bf16[1,128,128]{1,2,0:T(8,128)(2,1)S(1)} %copy.88) | copy-start | bytes 98308
  40.1 27.8 %all-to-all-start.1 = ((bf16[16,1,64,128]{3,2,1,0:T(8,128)(2,1)}), bf16[16,1,64,128]{3,2,1,0:T(8,128)(2,1)S(1)}, u32[]{:S(2)}, u32[]{:S(2)}) async-start(bf16[16,1,64,128]{3,2,1,0:T(8,128)(2,1)} %get-tuple-element.294), calls=%async_computation.1 | async-start | bytes 524288 | tf_op jit(solution)/shard_map/all_to_all | solution.py:31
  44.0 1.2 copy-start.3
  66.1 1.0 copy-start.4
  66.1 1.0 copy-start.12
  66.2 1.0 copy-start.16
  67.2 2.3 copy-start.6
  67.2 2.3 copy-start.8
  68.3 0.8 copy-start.1
  90.8 1.0 copy-start.2
  90.8 1.0 copy-start.13
  92.5 25.2 %copy-start.9 = (bf16[1,128,128]{2,1,0:T(8,128)(2,1)S(1)}, bf16[1,128,128]{2,1,0:T(8,128)(2,1)}, u32[]{:S(2)}) copy-start(bf16[1,128,128]{2,1,0:T(8,128)(2,1)} %param.36) | copy-start | bytes 98308
  92.5 25.3 %copy-start.10 = (bf16[1,128,128]{2,1,0:T(8,128)(2,1)S(1)}, bf16[1,128,128]{2,1,0:T(8,128)(2,1)}, u32[]{:S(2)}) copy-start(bf16[1,128,128]{2,1,0:T(8,128)(2,1)} %param.37) | copy-start | bytes 98308
  92.5 25.4 %copy-start.11 = (bf16[1,128,128]{2,1,0:T(8,128)(2,1)S(1)}, bf16[1,128,128]{2,1,0:T(8,128)(2,1)}, u32[]{:S(2)}) copy-start(bf16[1,128,128]{2,1,0:T(8,128)(2,1)} %param.38) | copy-start | bytes 98308
  94.1 58.3 %all-to-all-start.2 = ((bf16[512,1,1,2,1,1,2,128]{7,6,3,5,4,2,1,0:T(2,128)(2,1)}), bf16[512,1,1,2,1,1,2,128]{7,6,3,5,4,2,1,0:T(2,128)(2,1)S(1)}, u32[]{:S(2)}, u32[]{:S(2)}) async-start(bf16[512,1,1,2,1,1,2,128]{7,6,3,5,4,2,1,0:T(2,128)(2,1)} %copy.101), calls=%async_computation.2 | async-start | bytes 1048576 | tf_op jit(solution)/shard_map/all_to_all | solution.py:57
  206.7 1.3 copy-start.14
  206.7 1.3 copy-start.15
  206.7 1.3 copy-start.17
where the time goes:
time: 234 us; the launch traced here: 232 us
  waiting for transfers between devices  50.2 us (21%)
  local copies, waits for them, and re-layouts  47.5 us (20%)
  starting transfers between devices  45.5 us (19%)
  matrix products  42.5 us (18%)
  blocking collectives  22.4 us (10%)
  other arithmetic  22 us (9%)
    all_to_all x1, waiting for transfers between devices, one_exchange(): parts = lax.all_to_all(parts, axis, split_axis=0, concat_axis=0, tiled=True)  34.3 us
    squeeze x32, local copies, waits for them, and re-layouts, attend_heads(): results = lax.map(one_head, (query_heads, key_heads, value_heads))  24.5 us
    all_to_all x1, starting transfers between devices, one_exchange(): parts = lax.all_to_all(parts, axis, split_axis=0, concat_axis=0, tiled=True)  23.6 us
    all_to_all x2, blocking collectives, moved_by_axis(): whole = lax.all_to_all(whole, axes[k], k, k, tiled=True)  22.4 us
    all_to_all x2, starting transfers between devices, items_in_groups(): lax.all_to_all(group, axis, split_axis=split_dim, concat_axis=concat_dim,...  21.9 us
    dot_general x32, matrix products, one_block(): jnp.dot(weights, head_values, preferred_element_type=jnp.float32)  21.5 us
    reduce_sum x32, other arithmetic, one_block(): jnp.sum(expanded, axis=1, keepdims=True)  18.2 us
    dot_general x32, matrix products, one_block(): jnp.einsum('qd,kd->qk', block_queries, head_keys, preferred_element_type=...  16.9 us
  transfers between devices with their start and end apart: 3, of which 2 were waited for; matrix products, arithmetic and copies ran while one was open for 12% of the time, Pallas kernels for 0%

commit v1 on v0

v1 whole, which is shorter than its diff:
```python
import math

import jax
import jax.numpy as jnp
from jax import lax
from jax.experimental import pallas as pl
from jax.experimental.pallas import tpu as pltpu
from jax.sharding import Mesh
from jax.sharding import PartitionSpec as P

H = 4
C = 128
D = C // H
SCALE = math.log2(math.e) / math.sqrt(D)
ORIG = ("orig_0", "orig_1", "orig_2")
ORIG_DEST = ("orig_0", "orig_1", "orig_2", "dest")


epsilon = 1e-05
masked_score = -1e30


def items_in_groups(x, axis, split_dim, concat_dim, work, item_dim, out_dim):
    items = jax.tree.leaves(x)[0].shape[item_dim]
    count = 2 if items % 2 == 0 else 1
    finished = []
    for k in range(count):
        group = jax.tree.map(
            lambda a: lax.slice_in_dim(
                a, k * (items // count), (k + 1) * (items // count), axis=item_dim
            ),
            x,
        )
        finished.append(
            work(
                lax.all_to_all(
                    group, axis, split_axis=split_dim, concat_axis=concat_dim, tiled=True
                )
            )
        )
    return jax.tree.map(lambda *parts: jnp.concatenate(parts, axis=out_dim), *finished)


def in_blocks(x, dim, size):
    shape = x.shape
    parts = x.reshape(*shape[:dim], size, shape[dim] // size, *shape[dim + 1 :])
    return jnp.moveaxis(parts, dim, 0)


def laid_out(parts, dim):
    shape = list(parts.shape[1:])
    shape[dim] *= parts.shape[0]
    return jnp.moveaxis(parts, 0, dim).reshape(shape)


def one_exchange(x, axis, axes, splits, concats):
    sizes = [lax.axis_size(a) for a in axes]
    parts = in_blocks(x, splits[0], sizes[0])
    parts = jnp.moveaxis(in_blocks(parts, splits[1] + 1, sizes[1]), 0, 1)
    inside = parts.shape[2:]
    parts = parts.reshape(-1, *inside)
    parts = lax.all_to_all(parts, axis, split_axis=0, concat_axis=0, tiled=True)
    parts = laid_out(parts.reshape(*sizes, *inside), concats[0] + 1)
    return laid_out(parts, concats[1])


def moved_by_axis(parts, axes, order):
    inside = parts.shape[1:]
    whole = parts.reshape(*(lax.axis_size(a) for a in axes), *inside)
    for k in order:
        whole = lax.all_to_all(whole, axes[k], k, k, tiled=True)
    return whole.reshape(-1, *inside)


def core_and_chips(x, groups, order, split_dim, concat_dim):
    size = lax.axis_size(groups[0]) * lax.axis_size(groups[1])
    parts = in_blocks(x, split_dim, size)
    return laid_out(moved_by_axis(parts, groups, order), concat_dim)


def prepare(x, bias, w4_ref, gb_ref, kaug, qaug, vall, gates):
    wide = x.astype(jnp.float32)
    centered = wide - jnp.mean(wide, axis=-1, keepdims=True)
    variance = jnp.mean(centered * centered, axis=-1, keepdims=True)
    normed = (centered * lax.rsqrt(variance + epsilon)).astype(jnp.bfloat16)
    proj = jnp.dot(normed, w4_ref[...], preferred_element_type=jnp.float32)
    q = proj[:, :C].astype(jnp.bfloat16).astype(jnp.float32) * SCALE
    high = q.astype(jnp.bfloat16)
    low = (q - high.astype(jnp.float32)).astype(jnp.bfloat16)
    k = proj[:, C : 2 * C].astype(jnp.bfloat16)
    v = proj[:, 2 * C : 3 * C].astype(jnp.bfloat16)
    gates[...] = jax.nn.sigmoid(proj[:, 3 * C :] + gb_ref[...])
    n = x.shape[0]
    lane = lax.broadcasted_iota(jnp.int32, (n, C), 1)
    zero = jnp.zeros((n, C), jnp.bfloat16)
    one = jnp.ones((n, C), jnp.bfloat16)
    for h in range(H):
        mine = (lane >= D * h) & (lane < D * h + D)
        spot = lane == (D * h + D) % C
        qaug[h, :, :C] = jnp.where(mine, high, zero)
        qaug[h, :, C:] = jnp.where(spot, one, jnp.where(mine, low, zero))
        kaug[h, :, :C] = k
        kaug[h, :, C:] = jnp.where(spot, bias, k)
    vall[...] = v


def attend_item(x, kaug, qaug, vall, gates, wo_ref):
    heads = []
    for h in range(H):
        s = lax.dot_general(
            kaug[h], qaug[h], (((1,), (1,)), ((), ())), preferred_element_type=jnp.float32
        )
        p = jnp.exp2(s - jnp.max(s, axis=0, keepdims=True))
        w = (p * (1.0 / jnp.sum(p, axis=0, keepdims=True))).astype(jnp.bfloat16)
        heads.append(
            lax.dot_general(
                vall[:, D * h : D * h + D],
                w,
                (((0,), (0,)), ((), ())),
                preferred_element_type=jnp.float32,
            )
        )
    attended = jnp.concatenate(heads, axis=0).T.astype(jnp.bfloat16).astype(jnp.float32)
    gated = (gates[...] * attended).astype(jnp.bfloat16)
    update = jnp.dot(gated, wo_ref[...], preferred_element_type=jnp.float32)
    return (x.astype(jnp.float32) + update).astype(jnp.bfloat16)


def attend_kernel(x_ref, bias_ref, w4_ref, gb_ref, wo_ref, o_ref, kaug, qaug, vall, gates):
    prepare(x_ref[0], bias_ref[...], w4_ref, gb_ref, kaug, qaug, vall, gates)
    o_ref[0] = attend_item(x_ref[0], kaug, qaug, vall, gates, wo_ref)


def attend_pairs(x, weights, bias):
    w4, gate_bias, w_out = weights
    items, n, c = x.shape

    def whole(a):
        return pl.BlockSpec(a.shape, lambda i: (0,) * a.ndim)

    return pl.pallas_call(
        attend_kernel,
        grid=(items,),
        out_shape=jax.ShapeDtypeStruct(x.shape, jnp.bfloat16),
        in_specs=[
            pl.BlockSpec((1, n, c), lambda i: (i, 0, 0)),
            whole(bias),
            whole(w4),
            whole(gate_bias),
            whole(w_out),
        ],
        out_specs=pl.BlockSpec((1, n, c), lambda i: (i, 0, 0)),
        scratch_shapes=[
            pltpu.VMEM((H, n, 2 * c), jnp.bfloat16),
            pltpu.VMEM((H, n, 2 * c), jnp.bfloat16),
            pltpu.VMEM((n, c), jnp.bfloat16),
            pltpu.VMEM((n, c), jnp.float32),
        ],
        cost_estimate=pl.CostEstimate(
            flops=items * n * n * c * 8, bytes_accessed=items * n * c * 4, transcendentals=items * n * n * H
        ),
    )(x, bias, w4, gate_bias, w_out)


def body(
    pair_field,
    region_mask,
    region_count,
    row_query,
    row_key,
    row_value,
    row_gate,
    row_gate_bias,
    row_out,
    col_query,
    col_key,
    col_value,
    col_gate,
    col_gate_bias,
    col_out,
):
    tile_rows, tile_cols, channels = pair_field.shape
    dest_size = lax.axis_size("dest")
    orig_size = lax.axis_size(ORIG)
    region_total = region_mask.shape[0]
    row_part = tile_rows // dest_size
    col_part = tile_cols // orig_size
    positions = jnp.arange(region_total, dtype=jnp.int32)
    valid_keys = ((region_mask == 1) | (positions == 0)) & (positions < region_count[0])
    current = pair_field
    bias = jnp.broadcast_to(
        jnp.where(valid_keys, 0.0, masked_score).astype(jnp.bfloat16)[:, None],
        (region_total, channels),
    )
    row_weights = (
        jnp.concatenate((row_query[0], row_key[0], row_value[0], row_gate[0]), axis=1),
        row_gate_bias,
        row_out[0],
    )
    col_weights = (
        jnp.concatenate((col_query[0], col_key[0], col_value[0], col_gate[0]), axis=1),
        col_gate_bias,
        col_out[0],
    )

    def row_local(exchanged):
        return attend_pairs(exchanged[0], row_weights, bias)[None]

    pieces = current.reshape(dest_size, row_part, tile_cols, channels)
    rows_whole = items_in_groups(pieces, "dest", 0, 2, row_local, 1, 1)
    spread = rows_whole.reshape(1, 1, row_part, dest_size, orig_size, col_part, channels)
    columns = one_exchange(spread, ORIG_DEST, (ORIG, "dest"), (4, 3), (0, 1))
    column_columns = columns.reshape(region_total, col_part, channels)
    updated = jnp.swapaxes(
        attend_pairs(jnp.swapaxes(column_columns, 0, 1), col_weights, bias), 0, 1
    )
    back = core_and_chips(
        updated.reshape(region_total, 1, col_part, channels),
        (("orig_0", "orig_1"), "orig_2"),
        (1, 0),
        0,
        1,
    )
    current = back.reshape(tile_rows, tile_cols, channels)
    return current


def solution(mesh):
    split = Mesh(
        mesh.devices.reshape(4, 4, 2, mesh.shape["dest"]), ("orig_0", "orig_1", "orig_2", "dest")
    )
    return jax.shard_map(
        body,
        mesh=split,
        in_specs=(
            P(ORIG, "dest", None),
            P(),
            P(),
            P(),
            P(),
            P(),
            P(),
            P(),
            P(),
            P(),
            P(),
            P(),
            P(),
            P(),
            P(),
        ),
        out_specs=P(ORIG, "dest", None),
        check_vma=False,
    )
```

time: 234 us -> 169 us (0.72)
  matrix products: 42.5 us -> 0 us
  blocking collectives: 22.4 us -> 60.6 us
  local copies, waits for them, and re-layouts: 47.5 us -> 10.3 us
  Pallas kernels: 0 us -> 34.3 us
  starting transfers between devices: 45.5 us -> 20.9 us
  other arithmetic: 22 us -> 1.39 us
  waiting for transfers between devices: 50.2 us -> 40.4 us
    dot_general x70 -> x0, matrix products: 42.5 us -> none  [the longest x32 21.5 us: one_block(): jnp.dot(weights, head_values, preferred_element_type=jnp.float32)]
    all_to_all x0 -> x1, blocking collectives: none -> 38.2 us  [items_in_groups(): lax.all_to_all(group, axis, split_axis=split_dim, concat_axis=concat_dim,...]
    pallas_call x0 -> x3, Pallas kernels: none -> 34.3 us  [attend_pairs(): pl.pallas_call(attend_kernel, grid=(items,), out_shape=jax.ShapeDtypeStru...]
    squeeze x32 -> x0, local copies, waits for them, and re-layouts: 24.5 us -> none  [attend_heads(): results = lax.map(one_head, (query_heads, key_heads, value_heads))]
    reduce_sum x38 -> x0, other arithmetic: 20.4 us -> none  [the longest x32 18.2 us: one_block(): jnp.sum(expanded, axis=1, keepdims=True)]
    all_to_all x2 -> x1, starting transfers between devices: 21.9 us -> 3.68 us  [items_in_groups(): lax.all_to_all(group, axis, split_axis=split_dim, concat_axis=concat_dim,...]
    all_to_all x2 -> x1, waiting for transfers between devices: 15.9 us -> 6.4 us  [items_in_groups(): lax.all_to_all(group, axis, split_axis=split_dim, concat_axis=concat_dim,...]
    all_to_all x1, starting transfers between devices: 23.6 us -> 17.2 us  [one_exchange(): parts = lax.all_to_all(parts, axis, split_axis=0, concat_axis=0, tiled=True)]
  transfers between devices with their start and end apart: 3 -> 2, of which waited for: 2 -> 2; matrix products, arithmetic and copies ran while one was open for 12% -> 2% of each run, Pallas kernels for 0% -> 5%
where the time goes in v1:
time: 169 us
  blocking collectives  60.6 us (36%)
  waiting for transfers between devices  40.4 us (24%)
  Pallas kernels  34.3 us (20%)
  starting transfers between devices  20.9 us (12%)
  local copies, waits for them, and re-layouts  10.3 us (6%)
    all_to_all x1, blocking collectives, items_in_groups(): lax.all_to_all(group, axis, split_axis=split_dim, concat_axis=concat_dim,...  38.2 us
    pallas_call x3, Pallas kernels, attend_pairs(): pl.pallas_call(attend_kernel, grid=(items,), out_shape=jax.ShapeDtypeStru...  34.3 us
    all_to_all x1, waiting for transfers between devices, one_exchange(): parts = lax.all_to_all(parts, axis, split_axis=0, concat_axis=0, tiled=True)  34 us
    all_to_all x2, blocking collectives, moved_by_axis(): whole = lax.all_to_all(whole, axes[k], k, k, tiled=True)  22.4 us
    all_to_all x1, starting transfers between devices, one_exchange(): parts = lax.all_to_all(parts, axis, split_axis=0, concat_axis=0, tiled=True)  17.2 us
    all_to_all x1, waiting for transfers between devices, items_in_groups(): lax.all_to_all(group, axis, split_axis=split_dim, concat_axis=concat_dim,...  6.4 us
    all_to_all x1, starting transfers between devices, items_in_groups(): lax.all_to_all(group, axis, split_axis=split_dim, concat_axis=concat_dim,...  3.68 us
  transfers between devices with their start and end apart: 2, of which 2 were waited for; matrix products, arithmetic and copies ran while one was open for 2% of the time, Pallas kernels for 5%

profile of v1, /device:TPU:1, one launch (start us, length us, event | category | flops | bytes accessed | tf_op | source)
XLA Modules:
  0.0 168.6 jit_solution(16860414845707965824)
XLA Ops:
  0.0 1.8 %fusion.2 = (bf16[16,1,64,128]{3,2,1,0:T(8,128)(2,1)S(1)}, bf16[16,1,64,128]{3,2,1,0:T(8,128)(2,1)}) fusion(bf16[16,2,64,128]{3,2,1,0:T(8,128)(2,1)} %bitcast.45), kind=kLoop, calls=%fused_computation.8 | loop fusion | bytes 1048576 | tf_op jit(solution)/shard_map/slice | solution.py:29
  1.8 38.2 %all_to_all.33 = bf16[16,1,64,128]{3,2,1,0:T(8,128)(2,1)} all-to-all(bf16[16,1,64,128]{3,2,1,0:T(8,128)(2,1)S(1)} %get-tuple-element.5), channel_id=1, replica_groups=mesh['orig_0'=4,'orig_1'=4,'orig_2'=2,'dest'=16] {'dest'}, dimensions={0} | all-to-all | bytes 524288 | tf_op jit(solution)/shard_map/all_to_all | solution.py:36
  39.9 3.7 %all-to-all-start.1 = ((bf16[16,1,64,128]{3,2,1,0:T(8,128)(2,1)}), bf16[16,1,64,128]{3,2,1,0:T(8,128)(2,1)S(1)}, u32[]{:S(2)}, u32[]{:S(2)}) async-start(bf16[16,1,64,128]{3,2,1,0:T(8,128)(2,1)} %get-tuple-element.6), calls=%async_computation.1 | async-start | bytes 524288 | tf_op jit(solution)/shard_map/all_to_all | solution.py:36
  44.3 0.7 pad_maximum_fusion.1.w4_ref
  45.0 0.9 broadcast_in_dim.18.bias_ref
  45.9 9.0 %shard_map.145 = bf16[1,1024,128]{2,1,0:T(8,128)(2,1)} custom-call(bf16[1,1024,128]{2,1,0:T(8,128)(2,1)} %bitcast.49, bf16[1024,128]{1,0:T(8,128)(2,1)} %broadcast_in_dim.18.bias_ref, bf16[128,512]{1,0:T(8,128)(2,1)} %pad_maximum_fusion.1.w4_ref, f32[1,128]{1,0:T(1,128)} %gb_ref.4, bf16[128,128]{1,0:T(8,128)(2,1)} %bitcast.60), custom_call_target="tpu_custom_call" | custom-call | flops 1073741824 | bytes 524288 | tf_op jit(solution)/shard_map/pallas_call | solution.py:141
  54.9 1.1 copy.31
  56.0 6.4 %all-to-all-done.1 = bf16[16,1,64,128]{3,2,1,0:T(8,128)(2,1)S(1)} async-done(((bf16[16,1,64,128]{3,2,1,0:T(8,128)(2,1)}), bf16[16,1,64,128]{3,2,1,0:T(8,128)(2,1)S(1)}, u32[]{:S(2)}, u32[]{:S(2)}) %all-to-all-start.1) | async-done | bytes 262176 | tf_op jit(solution)/shard_map/all_to_all | solution.py:36
  62.4 0.7 copy-done
  63.1 9.1 %shard_map.146 = bf16[1,1024,128]{2,1,0:T(8,128)(2,1)} custom-call(bf16[1,1024,128]{2,1,0:T(8,128)(2,1)} %bitcast.48, bf16[1024,128]{1,0:T(8,128)(2,1)} %broadcast_in_dim.18.bias_ref, bf16[128,512]{1,0:T(8,128)(2,1)} %pad_maximum_fusion.1.w4_ref, f32[1,128]{1,0:T(1,128)} %gb_ref.4, bf16[128,128]{1,0:T(8,128)(2,1)} %bitcast.61), custom_call_target="tpu_custom_call" | custom-call | flops 1073741824 | bytes 524288 | tf_op jit(solution)/shard_map/pallas_call | solution.py:141
  72.2 1.1 copy.32
  73.4 0.1 pad_maximum_fusion
  73.4 1.3 copy.33
  74.8 17.2 %all-to-all-start.2 = ((bf16[512,1,1,2,1,1,2,128]{7,6,3,5,4,2,1,0:T(2,128)(2,1)}), bf16[512,1,1,2,1,1,2,128]{7,6,3,5,4,2,1,0:T(2,128)(2,1)S(1)}, u32[]{:S(2)}, u32[]{:S(2)}) async-start(bf16[512,1,1,2,1,1,2,128]{7,6,3,5,4,2,1,0:T(2,128)(2,1)} %copy.33), calls=%async_computation.2 | async-start | bytes 1048576 | tf_op jit(solution)/shard_map/all_to_all | solution.py:62
  92.0 0.7 pad_maximum_fusion.2.w4_ref
  92.7 34.0 %all-to-all-done.2 = bf16[512,1,1,2,1,1,2,128]{7,6,3,5,4,2,1,0:T(2,128)(2,1)S(1)} async-done(((bf16[512,1,1,2,1,1,2,128]{7,6,3,5,4,2,1,0:T(2,128)(2,1)}), bf16[512,1,1,2,1,1,2,128]{7,6,3,5,4,2,1,0:T(2,128)(2,1)S(1)}, u32[]{:S(2)}, u32[]{:S(2)}) %all-to-all-start.2) | async-done | bytes 524320 | tf_op jit(solution)/shard_map/all_to_all | solution.py:62
  126.7 1.1 copy.34
  127.8 16.2 %shard_map.147 = bf16[2,1024,128]{2,1,0:T(8,128)(2,1)} custom-call(bf16[2,1024,128]{2,1,0:T(8,128)(2,1)} %bitcast.46, bf16[1024,128]{1,0:T(8,128)(2,1)} %broadcast_in_dim.18.bias_ref, bf16[128,512]{1,0:T(8,128)(2,1)} %pad_maximum_fusion.2.w4_ref, f32[1,128]{1,0:T(1,128)} %gb_ref.5, bf16[128,128]{1,0:T(8,128)(2,1)} %bitcast.62), custom_call_target="tpu_custom_call" | custom-call | flops 2147483648 | bytes 1048576 | tf_op jit(solution)/shard_map/pallas_call | solution.py:141
  144.0 1.1 copy.35
  145.1 4.2 %all_to_all.34 = bf16[16,2,32,1,2,128]{5,2,0,4,3,1:T(8,128)(2,1)S(1)} all-to-all(bf16[16,2,32,1,2,128]{5,2,0,4,3,1:T(8,128)(2,1)S(1)} %copy.35), channel_id=1, replica_groups=mesh['orig_0'=4,'orig_1'=4,'orig_2'=2,'dest'=16] {'orig_2'}, dimensions={1} | all-to-all | bytes 1048576 | tf_op jit(solution)/shard_map/all_to_all | solution.py:71
  149.3 0.1 copy.36
  149.4 18.2 %all_to_all.35 = bf16[16,2,32,1,2,128]{5,2,1,4,3,0:T(8,128)(2,1)S(1)} all-to-all(bf16[16,2,32,1,2,128]{5,2,1,4,3,0:T(8,128)(2,1)S(1)} %copy.36), channel_id=1, replica_groups=mesh['orig_0'=4,'orig_1'=4,'orig_2'=2,'dest'=16] {'orig_0','orig_1'}, dimensions={0} | all-to-all | bytes 1048576 | tf_op jit(solution)/shard_map/all_to_all | solution.py:71
  167.6 0.1 copy.37
  167.6 1.0 copy.38
  (20 shorter events, 0.1 us)
Async XLA Ops:
  39.9 4.3 %copy-start.1 = (bf16[1,128,128]{2,1,0:T(8,128)(2,1)S(1)}, bf16[1,128,128]{2,1,0:T(8,128)(2,1)}, u32[]{:S(2)}) copy-start(bf16[1,128,128]{2,1,0:T(8,128)(2,1)} %param.21) | copy-start | bytes 98308
  39.9 4.4 %copy-start.2 = (bf16[1,128,128]{2,1,0:T(8,128)(2,1)S(1)}, bf16[1,128,128]{2,1,0:T(8,128)(2,1)}, u32[]{:S(2)}) copy-start(bf16[1,128,128]{2,1,0:T(8,128)(2,1)} %param.20) | copy-start | bytes 98308
  39.9 4.4 %copy-start.3 = (bf16[1,128,128]{2,1,0:T(8,128)(2,1)S(1)}, bf16[1,128,128]{2,1,0:T(8,128)(2,1)}, u32[]{:S(2)}) copy-start(bf16[1,128,128]{2,1,0:T(8,128)(2,1)} %param.19) | copy-start | bytes 98308
  39.9 4.4 %copy-start.4 = (bf16[1,128,128]{2,1,0:T(8,128)(2,1)S(1)}, bf16[1,128,128]{2,1,0:T(8,128)(2,1)}, u32[]{:S(2)}) copy-start(bf16[1,128,128]{2,1,0:T(8,128)(2,1)} %param.18) | copy-start | bytes 98308
  39.9 22.5 %all-to-all-start.1 = ((bf16[16,1,64,128]{3,2,1,0:T(8,128)(2,1)}), bf16[16,1,64,128]{3,2,1,0:T(8,128)(2,1)S(1)}, u32[]{:S(2)}, u32[]{:S(2)}) async-start(bf16[16,1,64,128]{3,2,1,0:T(8,128)(2,1)} %get-tuple-element.6), calls=%async_computation.1 | async-start | bytes 524288 | tf_op jit(solution)/shard_map/all_to_all | solution.py:36
  44.3 0.7 copy-start.9
  62.4 0.7 copy-start
  74.8 17.2 %copy-start.5 = (bf16[1,128,128]{2,1,0:T(8,128)(2,1)S(1)}, bf16[1,128,128]{2,1,0:T(8,128)(2,1)}, u32[]{:S(2)}) copy-start(bf16[1,128,128]{2,1,0:T(8,128)(2,1)} %param.27) | copy-start | bytes 98308
  74.8 17.2 %copy-start.6 = (bf16[1,128,128]{2,1,0:T(8,128)(2,1)S(1)}, bf16[1,128,128]{2,1,0:T(8,128)(2,1)}, u32[]{:S(2)}) copy-start(bf16[1,128,128]{2,1,0:T(8,128)(2,1)} %param.26) | copy-start | bytes 98308
  74.8 17.2 %copy-start.7 = (bf16[1,128,128]{2,1,0:T(8,128)(2,1)S(1)}, bf16[1,128,128]{2,1,0:T(8,128)(2,1)}, u32[]{:S(2)}) copy-start(bf16[1,128,128]{2,1,0:T(8,128)(2,1)} %param.25) | copy-start | bytes 98308
  74.8 17.2 %copy-start.8 = (bf16[1,128,128]{2,1,0:T(8,128)(2,1)S(1)}, bf16[1,128,128]{2,1,0:T(8,128)(2,1)}, u32[]{:S(2)}) copy-start(bf16[1,128,128]{2,1,0:T(8,128)(2,1)} %param.24) | copy-start | bytes 98308
  74.8 51.9 %all-to-all-start.2 = ((bf16[512,1,1,2,1,1,2,128]{7,6,3,5,4,2,1,0:T(2,128)(2,1)}), bf16[512,1,1,2,1,1,2,128]{7,6,3,5,4,2,1,0:T(2,128)(2,1)S(1)}, u32[]{:S(2)}, u32[]{:S(2)}) async-start(bf16[512,1,1,2,1,1,2,128]{7,6,3,5,4,2,1,0:T(2,128)(2,1)} %copy.33), calls=%async_computation.2 | async-start | bytes 1048576 | tf_op jit(solution)/shard_map/all_to_all | solution.py:62

commit v2 on v1

v2 whole, which is shorter than its diff:
```python
import math

import jax
import jax.numpy as jnp
from jax import lax
from jax.experimental import pallas as pl
from jax.experimental.pallas import tpu as pltpu
from jax.sharding import PartitionSpec as P

H = 4
C = 128
D = C // H
SCALE = math.log2(math.e) / math.sqrt(D)
epsilon = 1e-05
masked_score = -1e30
MESH = pl.DeviceIdType.MESH
BF16 = jnp.bfloat16


def prepare(x, bias, weights, kaug, qaug, vall, gates):
    wq_ref, wk_ref, wv_ref, wg_ref, gb_ref, _ = weights
    wide = x.astype(jnp.float32)
    centered = wide - jnp.mean(wide, axis=-1, keepdims=True)
    variance = jnp.mean(centered * centered, axis=-1, keepdims=True)
    normed = (centered * lax.rsqrt(variance + epsilon)).astype(jnp.bfloat16)

    def project(ref):
        return jnp.dot(normed, ref[...], preferred_element_type=jnp.float32)

    q = project(wq_ref).astype(jnp.bfloat16).astype(jnp.float32) * SCALE
    high = q.astype(jnp.bfloat16)
    low = (q - high.astype(jnp.float32)).astype(jnp.bfloat16)
    k = project(wk_ref).astype(jnp.bfloat16)
    v = project(wv_ref).astype(jnp.bfloat16)
    gates[...] = jax.nn.sigmoid(project(wg_ref) + gb_ref[...])
    n = x.shape[0]
    lane = lax.broadcasted_iota(jnp.int32, (n, C), 1)
    zero = jnp.zeros((n, C), jnp.bfloat16)
    one = jnp.ones((n, C), jnp.bfloat16)
    for h in range(H):
        mine = (lane >= D * h) & (lane < D * h + D)
        spot = lane == (D * h + D) % C
        qaug[h, :, :C] = jnp.where(mine, high, zero)
        qaug[h, :, C:] = jnp.where(spot, one, jnp.where(mine, low, zero))
        kaug[h, :, :C] = k
        kaug[h, :, C:] = jnp.where(spot, bias, k)
    vall[...] = v


def attend_item(x, kaug, qaug, vall, gates, wo_ref):
    heads = []
    for h in range(H):
        s = lax.dot_general(
            kaug[h], qaug[h], (((1,), (1,)), ((), ())), preferred_element_type=jnp.float32
        )
        p = jnp.exp2(s - jnp.max(s, axis=0, keepdims=True))
        w = (p * (1.0 / jnp.sum(p, axis=0, keepdims=True))).astype(jnp.bfloat16)
        heads.append(
            lax.dot_general(
                vall[:, D * h : D * h + D],
                w,
                (((0,), (0,)), ((), ())),
                preferred_element_type=jnp.float32,
            )
        )
    attended = jnp.concatenate(heads, axis=0).T.astype(jnp.bfloat16).astype(jnp.float32)
    gated = (gates[...] * attended).astype(jnp.bfloat16)
    update = jnp.dot(gated, wo_ref[...], preferred_element_type=jnp.float32)
    return (x.astype(jnp.float32) + update).astype(jnp.bfloat16)


def column_of(row):
    ones = jnp.ones((8, C), jnp.float32).astype(BF16)
    first = lax.broadcasted_iota(jnp.int32, (8, row.shape[1]), 0) == 0
    rows = jnp.where(first, jnp.broadcast_to(row, (8, row.shape[1])), 0.0).astype(BF16)
    return lax.dot_general(
        rows, ones, (((0,), (0,)), ((), ())), preferred_element_type=jnp.float32
    ).astype(BF16)


def permuted(matrix, x):
    return jnp.dot(matrix, x, preferred_element_type=jnp.float32).astype(BF16)


def whole_kernel(
    x_ref,
    mask_ref,
    count_ref,
    wq1,
    wk1,
    wv1,
    wg1,
    gb1,
    wo1,
    wq2,
    wk2,
    wv2,
    wg2,
    gb2,
    wo2,
    out_ref,
    rowbuf,
    rowres,
    zbuf,
    turned,
    colbuf,
    colres,
    homebuf,
    kaug,
    qaug,
    vall,
    gates,
    bias,
    swap,
    regroup,
    send_sem,
    recv_sem,
):
    o = lax.axis_index("orig")
    d = lax.axis_index("dest")
    zl, xc = o // 8, o % 8
    y, zh = d // 4, d % 4
    z = zh * 4 + zl
    across = (o + 16) % 32
    plane = xc * 4 + y

    def z_peer(t):
        zz = (z + t) % 16
        return (zz % 4) * 8 + xc, y * 4 + zz // 4

    def plane_peer(t):
        pp = (plane + t) % 32
        return zl * 8 + pp // 4, (pp % 4) * 4 + zh

    def home_peer(t):
        return (o + t) % 32, d

    barrier = pltpu.get_barrier_semaphore()

    def greet(peer, first, last):
        @pl.loop(first, last)
        def _(t):
            pl.semaphore_signal(barrier, inc=1, device_id=peer(t), device_id_type=MESH)

    greet(lambda t: (across, (d + t) % 16), 0, 16)
    greet(z_peer, 1, 16)
    greet(plane_peer, 1, 32)
    greet(home_peer, 1, 32)

    valid_row = (mask_ref[0:1] == 1) | (lax.broadcasted_iota(jnp.int32, (1, 1024), 1) == 0)
    valid_row = valid_row & (lax.broadcasted_iota(jnp.int32, (1, 1024), 1) < count_ref[0])
    bias[0] = column_of(jnp.where(valid_row, 0.0, masked_score))
    valid_col = (mask_ref[1:2] == 1) | (mask_ref[2:3] == 0)
    valid_col = valid_col & (mask_ref[2:3] < count_ref[0])
    bias[1] = column_of(jnp.where(valid_col, 0.0, masked_score))
    to = lax.broadcasted_iota(jnp.int32, (256, 256), 0)
    source = lax.broadcasted_iota(jnp.int32, (256, 256), 1)
    swap[...] = jnp.where(source == (to & 15) * 16 + (to >> 4), 1.0, 0.0).astype(BF16)
    regroup[...] = jnp.where(
        source == (to & 192) + ((to >> 2) & 3) * 16 + ((to >> 4) & 3) * 4 + (to & 3), 1.0, 0.0
    ).astype(BF16)

    pl.semaphore_wait(barrier, 16 + 15 + 31 + 31)

    def put(src, dst, stage, part, peer):
        pltpu.make_async_remote_copy(
            src_ref=src,
            dst_ref=dst,
            send_sem=send_sem.at[stage, part],
            recv_sem=recv_sem.at[stage, part],
            device_id=peer,
            device_id_type=MESH,
        ).start()

    def waiting(ref, stage, part):
        return pltpu.make_async_remote_copy(
            src_ref=ref,
            dst_ref=ref,
            send_sem=send_sem.at[stage, part],
            recv_sem=recv_sem.at[stage, part],
            device_id=(across, d),
            device_id_type=MESH,
        )

    def outwards(t):
        return 8 + ((t + 1) // 2) * (1 - 2 * (t % 2))

    for r in range(2):

        @pl.loop(0, 16)
        def _(t):
            to_d = (d + t) % 16
            put(x_ref.at[to_d, r], rowbuf.at[r, d], 0, r, (across, to_d))

    @pl.loop(0, 2)
    def _(r):
        waiting(rowbuf.at[r], 0, r).wait_recv()
        x = rowbuf[r].reshape(1024, C)
        prepare(x, bias[0], (wq1, wk1, wv1, wg1, gb1, wo1), kaug, qaug, vall, gates)
        rowres[r] = attend_item(x, kaug, qaug, vall, gates, wo1).reshape(4, 4, 4, 16, C)

        @pl.loop(0, 15)
        def _(t):
            zz = (z + outwards(t)) % 16
            put(
                rowres.at[r, :, zz // 4, zz % 4],
                zbuf.at[r, :, zl * 4 + zh],
                1,
                r,
                ((zz % 4) * 8 + xc, y * 4 + zz // 4),
            )

        zbuf[r, :, zl * 4 + zh] = rowres[r, :, zh, zl]

    @pl.loop(0, 2)
    def _(r):
        waiting(zbuf.at[r, :, 0:15], 1, r).wait_recv()
        for yy in range(4):
            turned[r, yy] = permuted(swap[...], zbuf[r, yy].reshape(256, C)).reshape(8, 2, 16, C)

        @pl.loop(1, 32)
        def _(t):
            pp = (plane + t) % 32
            put(
                turned.at[r, pp % 4, pp // 4],
                colbuf.at[:, r, plane],
                2,
                r,
                (zl * 8 + pp // 4, (pp % 4) * 4 + zh),
            )

        colbuf[:, r, plane] = turned[r, y, xc]

    for r in range(2):
        waiting(colbuf.at[:, r, 0:31], 2, r).wait_recv()

    @pl.loop(0, 2)
    def _(b):
        x = colbuf[b].reshape(1024, C)
        prepare(x, bias[1], (wq2, wk2, wv2, wg2, gb2, wo2), kaug, qaug, vall, gates)
        done = attend_item(x, kaug, qaug, vall, gates, wo2)
        for part in range(4):
            colres[b, part // 2, 4 * (part % 2) : 4 * (part % 2) + 4] = permuted(
                regroup[...], done[256 * part : 256 * part + 256]
            ).reshape(4, 4, 16, C)

        @pl.loop(1, 32)
        def _(t):
            oo = (o + t) % 32
            put(
                colres.at[b, :, oo % 8, (oo // 8 + 2) % 4],
                homebuf.at[:, o, b],
                3,
                b,
                (oo, d),
            )

        homebuf[:, o, b] = colres[b, :, xc, (zl + 2) % 4]

    for b in range(2):
        waiting(homebuf.at[:, 0:31, b], 3, b).wait_recv()
    for r in range(2):
        for q in range(4):
            out_ref[:, r, 16 * q : 16 * q + 16] = permuted(
                swap[...], homebuf[r, 8 * q : 8 * q + 8].reshape(256, C)
            ).reshape(16, 16, C)
    for part in range(2):
        waiting(rowbuf.at[part], 0, part).wait_send()
        waiting(zbuf.at[part, :, 0:15], 1, part).wait_send()
        waiting(colbuf.at[:, part, 0:31], 2, part).wait_send()
        waiting(homebuf.at[:, 0:31, part], 3, part).wait_send()


def body(pair_field, region_mask, region_count, *weights):
    weights = [w if w.ndim == 2 else w[0] for w in weights]
    positions = jnp.arange(1024, dtype=jnp.int32)

    def by_column_owner(a):
        parts = a.reshape(4, 8, 4, 4, 2)
        parts = jnp.concatenate((parts[2:], parts[:2]), axis=0)
        return jnp.transpose(parts, (4, 1, 2, 0, 3)).reshape(1024)

    masks = jnp.stack((region_mask, by_column_owner(region_mask), by_column_owner(positions)))
    vmem = pl.BlockSpec(memory_space=pltpu.VMEM)
    out = pl.pallas_call(
        whole_kernel,
        out_shape=jax.ShapeDtypeStruct((16, 2, 64, C), BF16),
        in_specs=[vmem, vmem, pl.BlockSpec(memory_space=pltpu.SMEM)] + [vmem] * 12,
        out_specs=vmem,
        scratch_shapes=[
            pltpu.VMEM((2, 16, 64, C), BF16),
            pltpu.VMEM((2, 4, 4, 4, 16, C), BF16),
            pltpu.VMEM((2, 4, 16, 16, C), BF16),
            pltpu.VMEM((2, 4, 8, 2, 16, C), BF16),
            pltpu.VMEM((2, 2, 32, 16, C), BF16),
            pltpu.VMEM((2, 2, 8, 4, 16, C), BF16),
            pltpu.VMEM((2, 32, 2, 16, C), BF16),
            pltpu.VMEM((H, 1024, 2 * C), BF16),
            pltpu.VMEM((H, 1024, 2 * C), BF16),
            pltpu.VMEM((1024, C), BF16),
            pltpu.VMEM((1024, C), jnp.float32),
            pltpu.VMEM((2, 1024, C), BF16),
            pltpu.VMEM((256, 256), BF16),
            pltpu.VMEM((256, 256), BF16),
            pltpu.SemaphoreType.DMA((4, 2)),
            pltpu.SemaphoreType.DMA((4, 2)),
        ],
        compiler_params=pltpu.CompilerParams(
            collective_id=0, has_side_effects=True, vmem_limit_bytes=60 * 1024 * 1024
        ),
    )(pair_field.reshape(16, 2, 64, C), masks, region_count, *weights)
    return out.reshape(32, 64, C)


def solution(mesh):
    tile = P("orig", "dest", None)
    return jax.shard_map(
        body,
        mesh=mesh,
        in_specs=(tile,) + (P(),) * 14,
        out_specs=tile,
        check_vma=False,
    )
```

time: 169 us -> 103 us (0.61)
  Pallas kernels: 34.3 us -> 97.3 us
  blocking collectives: 60.6 us -> 0 us
  waiting for transfers between devices: 40.4 us -> 0 us
  starting transfers between devices: 20.9 us -> 0 us
  local copies, waits for them, and re-layouts: 10.3 us -> 4.14 us
    pallas_call x3 -> x1, Pallas kernels: 34.3 us -> 97.3 us  [body(): pl.pallas_call(whole_kernel, out_shape=jax.ShapeDtypeStruct((16, 2, 64, C...]
    all_to_all x3 -> x0, blocking collectives: 60.6 us -> none  [the longest x1 38.2 us: items_in_groups(): lax.all_to_all(group, axis, split_axis=split_dim, concat_axis=concat_dim,...]
    all_to_all x2 -> x0, waiting for transfers between devices: 40.4 us -> none  [the longest x1 34 us: one_exchange(): parts = lax.all_to_all(parts, axis, split_axis=0, concat_axis=0, tiled=True)]
    all_to_all x2 -> x0, starting transfers between devices: 20.9 us -> none  [the longest x1 17.2 us: one_exchange(): parts = lax.all_to_all(parts, axis, split_axis=0, concat_axis=0, tiled=True)]
    reshape x2 -> x0, local copies, waits for them, and re-layouts: 2.43 us -> none  [the longest x1 1.33 us: one_exchange(): parts = parts.reshape(-1, *inside)]
    concatenate x2 -> x0, local copies, waits for them, and re-layouts: 2.25 us -> none  [items_in_groups(): jnp.concatenate(parts, axis=out_dim)]
    unnamed x20 -> x3, local copies, waits for them, and re-layouts: 0.75 us -> 2.55 us
    another operation x2, local copies, waits for them, and re-layouts: 2.08 us -> 0.33 us  [body(): jnp.stack((region_mask, by_column_owner(region_mask), by_column_owner(pos...]
  transfers between devices with their start and end apart: 2 -> 0, of which waited for: 2 -> 0; matrix products, arithmetic and copies ran while one was open for 2% -> 0% of each run, Pallas kernels for 5% -> 0%
where the time goes in v2:
time: 103 us
  Pallas kernels  97.3 us (94%)
  local copies, waits for them, and re-layouts  4.14 us (4%)
    pallas_call x1, Pallas kernels, body(): pl.pallas_call(whole_kernel, out_shape=jax.ShapeDtypeStruct((16, 2, 64, C...  97.3 us
    unnamed x3, local copies, waits for them, and re-layouts  2.55 us

profile of v2, /device:TPU:1, one launch (start us, length us, event | category | flops | bytes accessed | tf_op | source)
XLA Modules:
  0.0 102.9 jit_solution(14316072920440280348)
XLA Ops:
  0.7 0.0 copy-start
  0.7 0.7 copy-done
  1.3 0.2 slice.35
  1.6 0.3 copy.17
  1.8 0.2 slice.37
  2.0 0.3 copy.18
  2.3 0.3 copy.19
  2.6 0.2 stack_reshape.6
  2.8 0.1 fusion
  2.9 0.1 add_bitcast_fusion
  2.9 0.2 stack_reshape.7
  3.1 0.6 pad_add_fusion.mask_ref
  3.7 97.3 %shard_map.145 = bf16[16,2,64,128]{3,2,1,0:T(8,128)(2,1)} custom-call(bf16[16,2,64,128]{3,2,1,0:T(8,128)(2,1)} %bitcast.18, s32[3,1024]{1,0:T(4,128)} %pad_add_fusion.mask_ref, s32[1]{0:T(128)S(6)} %copy.21.count_ref, bf16[128,128]{1,0:T(8,128)(2,1)} %bitcast.19, bf16[128,128]{1,0:T(8,128)(2,1)} %bitcast.20, bf16[128,128]{1,0:T(8,128)(2,1)} %bitcast.21, ...), custom_call_target="tpu_custom_call" | custom-call | tf_op jit(solution)/shard_map/pallas_call | solution.py:285
  101.0 1.9 %copy.22 = bf16[32,64,128]{2,1,0:T(8,128)(2,1)} copy(bf16[32,64,128]{2,1,0:T(8,128)(2,1)} %bitcast.17) | data formatting | bytes 1048576
  (3 shorter events, 0.0 us)
Async XLA Ops:
  0.7 0.7 copy-start
